TPU v7x, 768 devices: a whole 4x8x12 slice. The times are simulated.
768 devices in a mesh: dp: 32 (over y, x), seq: 4 (over z_hi), tensor: 6 (over z_lo, core).
Axes of the slice: x: 4, y: 8, z: 12 (z_hi: 4, z_lo: 3; z = z_hi * 3 + z_lo), core: 2. Of those that a mesh axis runs over, the one named last changes fastest.
Arguments:
- memory_in: bfloat16 [192, 588, 1024], P(('dp', 'tensor'), 'seq'), may hold values from -6 to 6
- norm_gain: float32 [1024], replicated, may hold values from 0.1 to 1.9
- qkv_weight: bfloat16 [1024, 1536], replicated, may hold values from -1 to 1
- out_weight: bfloat16 [512, 1024], replicated, may hold values from -0.25 to 0.25
- key_weight: bfloat16 [1024, 1024], replicated, may hold values from -0.1875 to 0.1875
- value_weight: bfloat16 [1024, 1024], replicated, may hold values from -0.1875 to 0.1875
- shift_offsets: int32 [192, 2], P(('dp', 'tensor')), may hold values from 1 to 6
- row_order: int32 [192, 588], P('dp'), may hold values from 0 to 587, each once within a row
Outputs:
- keys: bfloat16 [192, 588, 1024], P('dp', 'tensor', 'seq')
- values: bfloat16 [192, 588, 1024], P('dp', 'tensor', 'seq')
All inputs are finite; a program needn't handle non-finite values.
Results may differ from a plain program's by a relative error of at most 0.008.
Values may be sent and summed in bfloat16 or wider, within the bound.
A program may use at most 64 MiB of HBM per device.

v0:
```python
import jax
import jax.numpy as jnp
from jax import lax
from jax.sharding import PartitionSpec as P

HEADS = 16
HEAD_DIM = 32
GRID_H = 28
GRID_W = 21
WIN = 7


def shifted(block, axis, distance):
    devices = range(lax.axis_size(axis))
    route = [((i - distance) % len(devices), i) for i in devices]
    return lax.ppermute(block, axis, route)


def window_block(rolled, first_row, row_shift, col_shift, norm_gain, qkv_weight, out_weight):
    row_count = rolled.shape[0] // GRID_W
    attn_width = HEADS * HEAD_DIM
    win_rows = row_count // WIN
    win_cols = GRID_W // WIN
    x_float = rolled.astype(jnp.float32)
    row_mean = jnp.mean(x_float, axis=-1, keepdims=True)
    row_var = jnp.mean((x_float - row_mean) ** 2, axis=-1, keepdims=True)
    normed = ((x_float - row_mean) * lax.rsqrt(row_var + 1e-05) * norm_gain).astype(jnp.bfloat16)
    projected_qkv = jnp.dot(normed, qkv_weight, preferred_element_type=jnp.float32).astype(
        jnp.bfloat16
    )

    def windows(block):
        block = block.reshape(win_rows, WIN, win_cols, WIN, HEADS, HEAD_DIM)
        return block.transpose(0, 2, 4, 1, 3, 5).reshape(
            win_rows * win_cols, HEADS, WIN * WIN, HEAD_DIM
        )

    queries = windows(projected_qkv[:, :attn_width])
    keys_win = windows(projected_qkv[:, attn_width : 2 * attn_width])
    values_win = windows(projected_qkv[:, 2 * attn_width :])
    scores = jnp.einsum(
        "whqd,whkd->whqk", queries, keys_win, preferred_element_type=jnp.float32
    ) * HEAD_DIM ** (-0.5)
    row_ids = first_row + jnp.arange(row_count, dtype=jnp.int32)
    col_ids = jnp.arange(GRID_W, dtype=jnp.int32)
    wrap_row = (row_ids >= GRID_H - row_shift).astype(jnp.int32)
    wrap_col = (col_ids >= GRID_W - col_shift).astype(jnp.int32)
    labels = 2 * wrap_row[:, None] + wrap_col[None, :]
    labels = (
        labels.reshape(win_rows, WIN, win_cols, WIN)
        .transpose(0, 2, 1, 3)
        .reshape(win_rows * win_cols, WIN * WIN)
    )
    same_region = labels[:, :, None] == labels[:, None, :]
    scores = jnp.where(same_region[:, None], scores, -1000000000.0)
    weights = jax.nn.softmax(scores, axis=-1).astype(jnp.bfloat16)
    attended = jnp.einsum(
        "whqk,whkd->whqd", weights, values_win, preferred_element_type=jnp.float32
    ).astype(jnp.bfloat16)
    restored = attended.reshape(win_rows, win_cols, HEADS, WIN, WIN, HEAD_DIM)
    restored = restored.transpose(0, 3, 1, 4, 2, 5).reshape(row_count * GRID_W, attn_width)
    return (x_float + jnp.dot(restored, out_weight, preferred_element_type=jnp.float32)).astype(
        jnp.bfloat16
    )


def local(
    memory_in, norm_gain, qkv_weight, out_weight, key_weight, value_weight, shift_offsets, row_order
):
    page_count, band_rows, emb_width = memory_in.shape
    band_height = band_rows // GRID_W
    top_rows = memory_in[:, : (WIN - 1) * GRID_W]
    after_rows = shifted(top_rows, "seq", -1)
    extended = jnp.concatenate([memory_in, after_rows], axis=1)
    extended = extended.reshape(page_count, band_height + WIN - 1, GRID_W, emb_width)
    first_row = lax.axis_index("seq") * band_height

    def per_page(page_grid, shifts):
        rolled = lax.dynamic_slice_in_dim(page_grid, shifts[0], band_height, 0)
        rolled = jnp.roll(rolled, -shifts[1], axis=1).reshape(band_height * GRID_W, emb_width)
        return window_block(
            rolled, first_row, shifts[0], shifts[1], norm_gain, qkv_weight, out_weight
        )

    memory = jax.vmap(per_page)(extended, shift_offsets)
    n_seq = lax.axis_size("seq")
    n_tensor = lax.axis_size("tensor")
    kv_width = key_weight.shape[1]
    own_cols = kv_width // n_seq
    group_pages = n_tensor * page_count
    all_rows = row_order.shape[1]
    pos_dev = all_rows // n_tensor
    first_col = lax.axis_index("seq") * own_cols
    both_weight = jnp.concatenate(
        [
            lax.dynamic_slice_in_dim(key_weight, first_col, own_cols, 1),
            lax.dynamic_slice_in_dim(value_weight, first_col, own_cols, 1),
        ],
        axis=1,
    )
    own_order = lax.dynamic_slice_in_dim(row_order, lax.axis_index("tensor") * pos_dev, pos_dev, 1)
    page_ids = jnp.arange(group_pages, dtype=jnp.int32)
    tensor_pos = (page_ids // page_count)[:, None]
    page_pos = (page_ids % page_count)[:, None]
    band_ids = own_order // band_rows
    within = own_order % band_rows
    flat_index = (
        ((band_ids * n_tensor + tensor_pos) * page_count + page_pos) * band_rows + within
    ).reshape(-1)
    empty_rows = jnp.zeros((group_pages * pos_dev, emb_width), jnp.bfloat16)
    piece_flat = lax.all_gather(memory[None], ("seq", "tensor"), axis=0, tiled=True).reshape(
        -1, emb_width
    )
    inside = (flat_index >= 0) & (flat_index < piece_flat.shape[0])
    taken_rows = jnp.take(piece_flat, jnp.clip(flat_index, 0, piece_flat.shape[0] - 1), axis=0)
    picked = jnp.where(inside[:, None], taken_rows, empty_rows)
    projected = jnp.dot(picked, both_weight, preferred_element_type=jnp.float32)
    key_out = projected[:, :own_cols].astype(jnp.bfloat16).reshape(group_pages, pos_dev, own_cols)
    value_out = projected[:, own_cols:].astype(jnp.bfloat16).reshape(group_pages, pos_dev, own_cols)
    return (key_out, value_out)


def solution(mesh):
    placed = (
        P(("dp", "tensor"), "seq", None),
        P(),
        P(),
        P(),
        P(),
        P(),
        P(("dp", "tensor"), None),
        P("dp", None),
    )
    return jax.shard_map(
        local,
        mesh=mesh,
        in_specs=placed,
        out_specs=(P("dp", "tensor", "seq"), P("dp", "tensor", "seq")),
        check_vma=False,
    )
```

profile of v0, /device:TPU:1, one launch (start us, length us, event | category | flops | bytes accessed | tf_op | source)
XLA Modules:
  0.0 178.4 jit_solution(10234784288136732909)
XLA Ops:
  7.2 0.0 copy-start
  7.2 0.0 all-gather.4.cloned.1.call-start
  7.2 1.1 slice.28
  8.3 15.1 %collective-permute-start = (bf16[1,126,1024]{2,1,0:T(8,128)(2,1)S(1)}, bf16[1,126,1024]{2,1,0:T(8,128)(2,1)}, u32[]{:S(2)}, u32[]{:S(2)}) collective-permute-start(bf16[1,126,1024]{2,1,0:T(8,128)(2,1)S(1)} %slice.28), channel_id=1, source_target_pairs={{6,0},{12,6},{18,12},{0,18},{7,1},{13,7},{19,13},{1,19},{8,2},{14,... | collective-permute-start | bytes 774152 | tf_op jit(solution)/shard_map/ppermute | solution.py:16
  23.5 1.3 fusion.42
  26.1 0.1 add_bitcast_fusion
  28.2 0.1 eq.28
  28.9 0.1 broadcast_compare_fusion
  29.0 10.6 %collective-permute-done = bf16[1,126,1024]{2,1,0:T(8,128)(2,1)} collective-permute-done((bf16[1,126,1024]{2,1,0:T(8,128)(2,1)S(1)}, bf16[1,126,1024]{2,1,0:T(8,128)(2,1)}, u32[]{:S(2)}, u32[]{:S(2)}) %collective-permute-start) | collective-permute-done | bytes 258080 | tf_op jit(solution)/shard_map/ppermute | solution.py:16
  39.6 2.0 %pad_maximum_fusion = bf16[1,273,1024]{2,1,0:T(8,128)(2,1)} fusion(bf16[1,126,1024]{2,1,0:T(8,128)(2,1)} %collective-permute-done, bf16[1,147,1024]{2,1,0:T(8,128)(2,1)} %param.8), kind=kLoop, calls=%fused_computation.34 | loop fusion | flops 1118208 | bytes 1118208 | tf_op jit(solution)/shard_map/concatenate | solution.py:74
  41.5 4.2 %reshape.389 = bf16[1,13,21,1024]{3,0,2,1:T(2,128)(2,1)} reshape(bf16[1,273,1024]{2,1,0:T(8,128)(2,1)} %pad_maximum_fusion) | data formatting | bytes 1118208 | tf_op jit(solution)/shard_map/reshape | solution.py:75
  45.7 1.7 constant_dynamic-slice_fusion.2
  47.4 4.2 %fusion.37 = (f32[7,21]{1,0:T(8,128)S(1)}, f32[7,21,1024]{2,1,0:T(8,128)}, f32[1,7,21,1024]{3,0,2,1:T(1,128)}) fusion(s32[]{:T(128)} %bitcast.3, bf16[1,7,21,1024]{3,0,2,1:T(2,128)(2,1)S(1)} %constant_dynamic-slice_fusion.2), kind=kLoop, calls=%fused_computation.68 | loop fusion | flops 451437 | bytes 1505872 | tf_op jit(solution)/shard_map/vmap()/reduce_sum | solution.py:25
  51.6 0.0 copy-start.1
  51.6 0.1 div.29
  51.7 3.1 %fusion.21 = f32[147]{0:T(256)S(1)} fusion(f32[1,7,21,1024]{3,0,2,1:T(1,128)} %get-tuple-element.28, f32[147]{0:T(256)S(1)} %div.29), kind=kLoop, calls=%fused_computation.32 | loop fusion | flops 451437 | bytes 603288 | tf_op jit(solution)/shard_map/vmap()/reduce_sum | solution.py:26
  54.8 2.0 %reshape.373 = f32[147,1024]{1,0:T(8,128)} reshape(f32[7,21,1024]{2,1,0:T(8,128)} %get-tuple-element.25) | data formatting | bytes 1204224 | tf_op jit(solution)/shard_map/vmap()/convert_element_type | solution.py:24
  56.9 0.0 copy-done
  56.9 0.0 copy-done.1
  56.9 1.8 %fusion.1 = bf16[1,147,1536]{2,1,0:T(8,128)(2,1)S(1)} fusion(bf16[1024,1536]{1,0:T(8,128)(2,1)S(1)} %copy-done, f32[147,1024]{1,0:T(8,128)} %reshape.373, f32[1024]{0:T(1024)S(1)} %copy-done.1, f32[147]{0:T(256)S(1)} %add_rsqrt_fusion, f32[147]{0:T(256)S(1)} %div.29), kind=kOutput, calls=%fused_computation.3 | convolution fusion | flops 463249920 | bytes 4204696 | tf_op jit(solution)/shard_map/vmap()/dot_general | solution.py:28
  58.7 0.7 fusion.41
  59.4 2.1 %reshape.306 = bf16[1,1,7,3,7,16,32]{6,5,4,3,2,1,0:T(8,128)(2,1)} reshape(bf16[1,147,512]{2,1,0:T(8,128)(2,1)} %get-tuple-element.31) | data formatting | bytes 301056 | tf_op jit(solution)/shard_map/vmap()/reshape | solution.py:33
  61.5 1.9 %copy.25 = bf16[1,1,7,3,7,16,32]{6,5,4,2,3,1,0:T(8,128)(2,1)} copy(bf16[1,1,7,3,7,16,32]{6,5,4,3,2,1,0:T(8,128)(2,1)} %reshape.306) | data formatting | bytes 301056 | tf_op jit(solution)/shard_map/vmap()/reshape | solution.py:33
  63.4 1.1 reshape.308
  64.5 1.1 copy.26
  65.7 1.6 fusion.4
  67.3 0.0 copy-start.2
  67.3 1.1 copy-done.2
  68.4 1.0 fusion.43
  69.3 1.2 reshape.310
  70.5 1.9 %copy.29 = bf16[1,1,7,3,7,16,32]{6,5,4,2,3,1,0:T(8,128)(2,1)} copy(bf16[1,1,7,3,7,16,32]{6,5,4,3,2,1,0:T(8,128)(2,1)} %reshape.310) | data formatting | bytes 301056 | tf_op jit(solution)/shard_map/vmap()/reshape | solution.py:33
  72.4 2.5 %convolution_convert_fusion.2 = bf16[3,16,49,32]{2,3,1,0:T(8,128)(2,1)S(1)} fusion(bf16[3,16,49,32]{3,1,2,0:T(8,128)(2,1)} %bitcast.40, f32[3,16,49]{2,1,0:T(8,128)} %fusion.43, f32[3,16,49,49]{2,3,1,0:T(8,128)} %copy-done.2), kind=kOutput, calls=%fused_computation.11 | convolution fusion | flops 7799280 | bytes 771456 | tf_op jit(solution)/shard_map/vmap(whqk,whkd->whqd)/dot_general | solution.py:57
  75.0 1.3 copy.32
  76.3 1.9 %copy.33 = bf16[1,1,7,3,7,16,32]{6,5,4,3,2,1,0:T(8,128)(2,1)} copy(bf16[1,1,7,3,7,16,32]{6,5,4,2,3,1,0:T(8,128)(2,1)} %bitcast.37) | data formatting | bytes 301056 | tf_op jit(solution)/shard_map/vmap()/transpose | solution.py:61
  78.2 1.6 reshape.313
  79.8 2.5 %fusion.10 = bf16[1,147,1024]{2,1,0:T(8,128)(2,1)} fusion(f32[147,1024]{1,0:T(8,128)} %reshape.373, bf16[147,512]{1,0:T(8,128)(2,1)S(1)} %reshape.313, bf16[512,1024]{1,0:T(8,128)(2,1)} %param.11), kind=kOutput, calls=%fused_computation.19 | convolution fusion | flops 154441728 | bytes 2102272 | tf_op jit(solution)/shard_map/vmap()/dot_general | solution.py:62
  82.3 0.0 all-gather.4.cloned.1.call-update
  82.3 0.8 compare_and_fusion.1
  83.1 0.1 min.18
  83.2 0.1 min.16
  83.3 0.1 and.44
  83.4 2.3 %constant_dynamic-slice_fusion = (bf16[1024,256]{1,0:T(8,128)(2,1)}, bf16[1024,256]{1,0:T(8,128)(2,1)}) fusion(bf16[1024,1024]{1,0:T(8,128)(2,1)} %param.13, s32[]{:T(128)S(6)} %select_n.85, bf16[1024,1024]{1,0:T(8,128)(2,1)} %param.12), kind=kLoop, calls=%fused_computation.60 | loop fusion | bytes 2097156 | tf_op jit(solution)/shard_map/dynamic_slice | solution.py:97
  85.7 63.6 %all-gather.4.cloned.1.call-done = bf16[24,147,1024]{2,1,0:T(8,128)(2,1)} async-done(((bf16[1,147,1024]{2,1,0:T(8,128)(2,1)}), bf16[24,147,1024]{2,1,0:T(8,128)(2,1)}) %all-gather.4.cloned.1.call-update) | async-done | bytes 7225360 | tf_op jit(solution)/shard_map/all_gather | solution.py:111
  149.3 8.1 %reshape.388 = bf16[3528,1024]{1,0:T(8,128)(2,1)} reshape(bf16[24,147,1024]{2,1,0:T(8,128)(2,1)} %all-gather.4.cloned.1.call-done) | data formatting | bytes 14450688
  157.4 8.4 %gather_fusion = bf16[588,1024]{1,0:T(8,128)(2,1)} fusion(bf16[3528,1024]{1,0:T(8,128)(2,1)} %reshape.388, s32[1024]{0:T(1024)S(1)} %pad_clamp_fusion), kind=kCustom, calls=%fused_computation | custom fusion | bytes 2410800 | tf_op jit(solution)/shard_map/jit(_take)/gather | solution.py:115
  165.8 2.4 %convolution_convert_fusion.1 = bf16[588,512]{1,0:T(8,128)(2,1)S(1)} fusion(bf16[588,1024]{1,0:T(8,128)(2,1)} %gather_fusion, pred[588]{0:T(1024)(128)(4,1)S(1)} %compare_and_fusion, pred[588]{0:T(1024)(128)(4,1)S(1)} %and.44, bf16[1024,256]{1,0:T(8,128)(2,1)} %get-tuple-element.36, bf16[1024,256]{1,0:T(8,128)(2,1)} %get-tuple-element.37), kind=kOutput, calls=%fused_computation.9 | convolution fusion | flops 620165120 | bytes 2856088 | tf_op jit(solution)/shard_map/dot_general | solution.py:117
  168.2 0.8 fusion.40
  169.0 1.8 reshape.315
  170.7 0.8 reshape.316
  (8 shorter events, 0.1 us)
Async XLA Ops:
  7.2 49.7 %copy-start = (bf16[1024,1536]{1,0:T(8,128)(2,1)S(1)}, bf16[1024,1536]{1,0:T(8,128)(2,1)}, u32[]{:S(2)}) copy-start(bf16[1024,1536]{1,0:T(8,128)(2,1)} %param.10) | copy-start | bytes 9437188
  7.2 142.2 %all-gather.4.cloned.1.call-start = ((), (), s32[]{:S(2)}) async-start(), calls=%async_computation | async-start | bytes 7782400 | tf_op jit(solution)/shard_map/all_gather | solution.py:111
  8.3 31.2 %collective-permute-start = (bf16[1,126,1024]{2,1,0:T(8,128)(2,1)S(1)}, bf16[1,126,1024]{2,1,0:T(8,128)(2,1)}, u32[]{:S(2)}, u32[]{:S(2)}) collective-permute-start(bf16[1,126,1024]{2,1,0:T(8,128)(2,1)S(1)} %slice.28), channel_id=1, source_target_pairs={{6,0},{12,6},{18,12},{0,18},{7,1},{13,7},{19,13},{1,19},{8,2},{14,... | collective-permute-start | bytes 774152 | tf_op jit(solution)/shard_map/ppermute | solution.py:16
  51.6 5.2 %copy-start.1 = (f32[1024]{0:T(1024)S(1)}, f32[1024]{0:T(1024)}, u32[]{:S(2)}) copy-start(f32[1024]{0:T(1024)} %param.9) | copy-start | bytes 12292
  67.3 1.1 copy-start.2
Sparse Core Ops, SparseCore 0:
  82.4 66.8 all-gather.3
where the time goes:
time: 179 us; the launch traced here: 178 us
  waiting for transfers between devices  74.2 us (41%)
  local copies, waits for them, and re-layouts  48.9 us (27%)
  between operations  18.1 us (10%)
  starting transfers between devices  15.2 us (8%)
  other arithmetic  11.2 us (6%)
  matrix products  10.8 us (6%)
    all_gather x1, waiting for transfers between devices, local(): lax.all_gather(memory[None], ('seq', 'tensor'), axis=0, tiled=True)  63.6 us
    ppermute x1, starting transfers between devices, shifted(): return lax.ppermute(block, axis, route)  15.1 us
    ppermute x1, waiting for transfers between devices, shifted(): return lax.ppermute(block, axis, route)  10.6 us
    reshape x6, local copies, waits for them, and re-layouts, windows(): block = block.reshape(win_rows, WIN, win_cols, WIN, HEADS, HEAD_DIM)  9.38 us
    unnamed x7, local copies, waits for them, and re-layouts  9.16 us
    gather x1, local copies, waits for them, and re-layouts, local(): jnp.take(piece_flat, jnp.clip(flat_index, 0, piece_flat.shape[0] - 1), ax...  8.4 us
    reshape x1, local copies, waits for them, and re-layouts, local(): extended.reshape(page_count, band_height + WIN - 1, GRID_W, emb_width)  4.21 us
    reduce_sum x1, other arithmetic, window_block(): row_mean = jnp.mean(x_float, axis=-1, keepdims=True)  4.21 us
  transfers between devices with their start and end apart: 2, of which 2 were waited for; matrix products, arithmetic and copies ran while one was open for 3% of the time, Pallas kernels for 0%

commit v1 on v0

v1 whole, which is shorter than its diff:
```python
import functools

import jax
import jax.numpy as jnp
from jax import lax
from jax.experimental import pallas as pl
from jax.experimental.pallas import tpu as pltpu
from jax.sharding import PartitionSpec as P

HEADS = 16
HEAD_DIM = 32
GRID_H = 28
GRID_W = 21
WIN = 7
ATTN = HEADS * HEAD_DIM
SLOTS = 160
HALO = 64
TOP = 84
GAP = 12
MESH = pl.DeviceIdType.MESH
FAR_FIRST = (2, 1, 3)


def over_21(n):
    return (n * 3121) >> 16


def over_7(n):
    return (n * 9363) >> 16


def group_ids(slot, band, a, c):
    q = jnp.where(slot >= TOP + GAP, slot - GAP, slot)
    valid = (slot < TOP) | ((slot >= TOP + GAP) & (slot < SLOTS - 1))
    row = over_21(q)
    col = q - GRID_W * row
    across = jnp.where(col < c, col - c + GRID_W, col - c)
    wrap_row = jnp.where((row < a) & (band == 3), 2, 0)
    wrap_col = jnp.where(col < c, 1, 0)
    return jnp.where(valid, over_7(across) * 4 + wrap_row + wrap_col, -1)


def kernel(
    n_seq,
    n_tensor,
    shift_ref,
    x_ref,
    gain_ref,
    order_ref,
    qkv_hbm,
    out_hbm,
    key_hbm,
    value_hbm,
    k_out,
    v_out,
    xs,
    top_in,
    low_in,
    normed,
    wq,
    wo,
    wk,
    wv,
    qkv,
    bias,
    att,
    mem,
    k_send,
    v_send,
    k_all,
    v_all,
    chosen,
    k_turn,
    v_turn,
    load_sem,
    halo_send,
    halo_recv,
    seq_send,
    seq_recv,
    turn_send,
    turn_recv,
):
    s = lax.axis_index("seq")
    t = lax.axis_index("tensor")
    cols = k_out.shape[2]
    pos = k_out.shape[1]

    loads = [
        pltpu.make_async_copy(qkv_hbm, wq, load_sem.at[0]),
        pltpu.make_async_copy(out_hbm, wo, load_sem.at[1]),
    ]
    for r in range(n_seq):
        at = pl.ds(pl.multiple_of(lax.rem(s + r, n_seq) * cols, 128), cols)
        loads.append(pltpu.make_async_copy(key_hbm.at[:, at], wk.at[r], load_sem.at[2 + r]))
        loads.append(
            pltpu.make_async_copy(value_hbm.at[:, at], wv.at[r], load_sem.at[2 + n_seq + r])
        )
    for load in loads:
        load.start()

    barrier = pltpu.get_barrier_semaphore()
    for r in range(1, n_seq):
        pl.semaphore_signal(
            barrier, inc=1, device_id={"seq": lax.rem(s + r, n_seq)}, device_id_type=MESH
        )
    for r in range(1, n_tensor):
        pl.semaphore_signal(
            barrier, inc=1, device_id={"tensor": lax.rem(t + r, n_tensor)}, device_id_type=MESH
        )

    a = shift_ref[0, 0]
    c = shift_ref[0, 1]
    late = jnp.where(a >= 4, 1, 0)

    xs[TOP : TOP + GAP] = jnp.zeros((GAP, xs.shape[1]), xs.dtype)
    xs[pl.ds(SLOTS - 16, 16)] = jnp.zeros((16, xs.shape[1]), xs.dtype)
    xs[0:TOP] = x_ref[0:TOP]
    xs[TOP + GAP : SLOTS - 1] = x_ref[TOP : TOP + 63]

    pl.semaphore_wait(barrier, n_seq - 1 + n_tensor - 1)
    up = pltpu.make_async_remote_copy(
        src_ref=xs.at[0:HALO],
        dst_ref=top_in,
        send_sem=halo_send.at[0],
        recv_sem=halo_recv.at[0],
        device_id={"seq": lax.rem(s + n_seq - 1, n_seq)},
        device_id_type=MESH,
    )
    down = pltpu.make_async_remote_copy(
        src_ref=xs.at[SLOTS - HALO : SLOTS],
        dst_ref=low_in,
        send_sem=halo_send.at[1],
        recv_sem=halo_recv.at[1],
        device_id={"seq": lax.rem(s + 1, n_seq)},
        device_id_type=MESH,
    )
    up.start()
    down.start()

    band = lax.rem(s + n_seq - late, n_seq)
    ids_q = group_ids(lax.broadcasted_iota(jnp.int32, (SLOTS, SLOTS), 0), band, a, c)
    ids_k = group_ids(lax.broadcasted_iota(jnp.int32, (SLOTS, SLOTS), 1), band, a, c)
    bias[...] = jnp.where(ids_q == ids_k, 0.0, -1e9)

    order = order_ref[pl.ds(t, 1), :]
    r_row = over_21(order)
    r_col = order - GRID_W * r_row
    r_band = over_7(r_row)
    row = r_row - WIN * r_band + a
    row = jnp.where(row >= WIN, row - WIN, row)
    col = r_col + c
    col = jnp.where(col >= GRID_W, col - GRID_W, col)
    q = row * GRID_W + col
    slot = jnp.where(q >= TOP, q + GAP, q)
    source = (r_band + late) & (n_seq - 1)
    index = source * SLOTS + slot
    for i in range(n_tensor):
        part = index[:, i * pos : (i + 1) * pos]
        part = jnp.concatenate([part, jnp.full((1, 128 - pos), -1, jnp.int32)], axis=1)
        tall = jnp.transpose(jnp.broadcast_to(part, (8, 128)))[:, 0:1]
        places = lax.broadcasted_iota(jnp.int32, (128, n_seq * SLOTS), 1)
        chosen[i] = jnp.where(tall == places, 1.0, 0.0).astype(jnp.bfloat16)

    up.wait()
    down.wait()

    top_end = jnp.where(a <= 3, GRID_W * a, 0)
    low_start = jnp.where(a >= 4, GRID_W * a, 4096) + GAP
    slots_top = lax.broadcasted_iota(jnp.int32, (HALO, xs.shape[1]), 0)
    xs[0:HALO] = jnp.where(
        slots_top < top_end, top_in[...].astype(jnp.float32), xs[0:HALO].astype(jnp.float32)
    ).astype(jnp.bfloat16)
    xs[SLOTS - HALO : SLOTS] = jnp.where(
        slots_top + (SLOTS - HALO) >= low_start,
        low_in[...].astype(jnp.float32),
        xs[SLOTS - HALO : SLOTS].astype(jnp.float32),
    ).astype(jnp.bfloat16)

    def norm(i, carry):
        at = pl.ds(pl.multiple_of(i * 32, 32), 32)
        block = xs[at].astype(jnp.float32)
        mean = jnp.mean(block, axis=-1, keepdims=True)
        block = block - mean
        var = jnp.mean(block * block, axis=-1, keepdims=True)
        normed[at] = (block * lax.rsqrt(var + 1e-05) * gain_ref[...]).astype(jnp.bfloat16)
        return carry

    lax.fori_loop(0, SLOTS // 32, norm, 0)

    loads[0].wait()

    def project(i, carry):
        at = pl.ds(pl.multiple_of(i * 512, 512), 512)
        qkv[:, at] = jnp.dot(
            normed[...], wq[:, at], preferred_element_type=jnp.float32
        ).astype(jnp.bfloat16)
        return carry

    lax.fori_loop(0, 3, project, 0)

    lane_head = lax.broadcasted_iota(jnp.int32, (SLOTS, 128), 1) >> 5

    def attend(g, carry):
        start = pl.multiple_of(g * 128, 128)
        queries = qkv[:, pl.ds(start, 128)]
        keys = qkv[:, pl.ds(start + ATTN, 128)]
        values = qkv[:, pl.ds(start + 2 * ATTN, 128)]
        total = jnp.zeros((SLOTS, 128), jnp.float32)
        for h in range(4):
            own = jnp.where(lane_head == h, 1.0, 0.0).astype(jnp.bfloat16)
            scores = lax.dot_general(
                queries * own, keys, (((1,), (1,)), ((), ())), preferred_element_type=jnp.float32
            )
            scores = scores * HEAD_DIM ** (-0.5) + bias[...]
            top = jnp.max(scores, axis=-1, keepdims=True)
            weights = jnp.exp(scores - top)
            weights = weights / jnp.sum(weights, axis=-1, keepdims=True)
            got = jnp.dot(
                weights.astype(jnp.bfloat16), values, preferred_element_type=jnp.float32
            )
            total = jnp.where(lane_head == h, got, total)
        att[:, pl.ds(start, 128)] = total.astype(jnp.bfloat16)
        return carry

    lax.fori_loop(0, HEADS // 4, attend, 0)

    loads[1].wait()

    def outward(i, carry):
        at = pl.ds(pl.multiple_of(i * 512, 512), 512)
        mem[:, at] = (
            xs[:, at].astype(jnp.float32)
            + jnp.dot(att[...], wo[:, at], preferred_element_type=jnp.float32)
        ).astype(jnp.bfloat16)
        return carry

    lax.fori_loop(0, 2, outward, 0)

    def seq_copy(r, half, slot):
        sent, held = ((k_send, k_all), (v_send, v_all))[half]
        return pltpu.make_async_remote_copy(
            src_ref=sent.at[r - 1],
            dst_ref=held.at[slot],
            send_sem=seq_send.at[half, r - 1],
            recv_sem=seq_recv.at[half, r - 1],
            device_id={"seq": lax.rem(s + r, n_seq)},
            device_id_type=MESH,
        )

    for half, (weight, sent, held) in enumerate(((wk, k_send, k_all), (wv, v_send, v_all))):
        for r in FAR_FIRST:
            loads[2 + 2 * r + half].wait()
            sent[r - 1] = jnp.dot(
                mem[...], weight[r], preferred_element_type=jnp.float32
            ).astype(jnp.bfloat16)
            seq_copy(r, half, s).start()
        loads[2 + half].wait()
        held[s] = jnp.dot(mem[...], weight[0], preferred_element_type=jnp.float32).astype(
            jnp.bfloat16
        )

    def turn_copy(r, half, page):
        sent, held = ((k_turn, k_out), (v_turn, v_out))[half]
        return pltpu.make_async_remote_copy(
            src_ref=sent.at[r - 1],
            dst_ref=held.at[page],
            send_sem=turn_send.at[half, r - 1],
            recv_sem=turn_recv.at[half, r - 1],
            device_id={"tensor": lax.rem(t + r, n_tensor)},
            device_id_type=MESH,
        )

    for half, (held, sent, result) in enumerate(((k_all, k_turn, k_out), (v_all, v_turn, v_out))):
        for r in range(1, n_seq):
            seq_copy(r, half, lax.rem(s + n_seq - r, n_seq)).wait_recv()
        for r in range(1, n_tensor + 1):
            rows = jnp.dot(
                chosen[lax.rem(t + r, n_tensor)],
                held[...].reshape(n_seq * SLOTS, cols),
                preferred_element_type=jnp.float32,
            )[0:pos].astype(jnp.bfloat16)
            if r < n_tensor:
                sent[r - 1] = rows
                turn_copy(r, half, t).start()
            else:
                result[t] = rows

    for half in range(2):
        for r in range(1, n_seq):
            seq_copy(r, half, s).wait_send()
        for r in range(1, n_tensor):
            turn_copy(r, half, lax.rem(t + n_tensor - r, n_tensor)).wait()


def local(
    memory_in, norm_gain, qkv_weight, out_weight, key_weight, value_weight, shift_offsets, row_order
):
    n_seq = lax.axis_size("seq")
    n_tensor = lax.axis_size("tensor")
    width = memory_in.shape[2]
    cols = key_weight.shape[1] // n_seq
    pos = row_order.shape[1] // n_tensor
    bf16 = jnp.bfloat16
    vmem = pl.BlockSpec(memory_space=pltpu.VMEM)
    away = pl.BlockSpec(memory_space=pl.ANY)
    out = jax.ShapeDtypeStruct((n_tensor, pos, cols), bf16)
    return pl.pallas_call(
        functools.partial(kernel, n_seq, n_tensor),
        out_shape=(out, out),
        in_specs=[
            pl.BlockSpec(memory_space=pltpu.SMEM),
            vmem,
            vmem,
            vmem,
            away,
            away,
            away,
            away,
        ],
        out_specs=(vmem, vmem),
        scratch_shapes=[
            pltpu.VMEM((SLOTS, width), bf16),
            pltpu.VMEM((HALO, width), bf16),
            pltpu.VMEM((HALO, width), bf16),
            pltpu.VMEM((SLOTS, width), bf16),
            pltpu.VMEM((width, 3 * ATTN), bf16),
            pltpu.VMEM((ATTN, width), bf16),
            pltpu.VMEM((n_seq, width, cols), bf16),
            pltpu.VMEM((n_seq, width, cols), bf16),
            pltpu.VMEM((SLOTS, 3 * ATTN), bf16),
            pltpu.VMEM((SLOTS, SLOTS), jnp.float32),
            pltpu.VMEM((SLOTS, ATTN), bf16),
            pltpu.VMEM((SLOTS, width), bf16),
            pltpu.VMEM((n_seq - 1, SLOTS, cols), bf16),
            pltpu.VMEM((n_seq - 1, SLOTS, cols), bf16),
            pltpu.VMEM((n_seq, SLOTS, cols), bf16),
            pltpu.VMEM((n_seq, SLOTS, cols), bf16),
            pltpu.VMEM((n_tensor, 128, n_seq * SLOTS), bf16),
            pltpu.VMEM((n_tensor - 1, pos, cols), bf16),
            pltpu.VMEM((n_tensor - 1, pos, cols), bf16),
            pltpu.SemaphoreType.DMA((2 + 2 * n_seq,)),
            pltpu.SemaphoreType.DMA((2,)),
            pltpu.SemaphoreType.DMA((2,)),
            pltpu.SemaphoreType.DMA((2, n_seq - 1)),
            pltpu.SemaphoreType.DMA((2, n_seq - 1)),
            pltpu.SemaphoreType.DMA((2, n_tensor - 1)),
            pltpu.SemaphoreType.DMA((2, n_tensor - 1)),
        ],
        compiler_params=pltpu.CompilerParams(
            collective_id=0, has_side_effects=True, vmem_limit_bytes=60 * 1024 * 1024
        ),
        name="encode_to_kv",
    )(
        shift_offsets,
        memory_in.reshape(memory_in.shape[1:]),
        norm_gain.reshape(1, width),
        row_order,
        qkv_weight,
        out_weight,
        key_weight,
        value_weight,
    )


def solution(mesh):
    placed = (
        P(("dp", "tensor"), "seq", None),
        P(),
        P(),
        P(),
        P(),
        P(),
        P(("dp", "tensor"), None),
        P("dp", None),
    )
    return jax.shard_map(
        local,
        mesh=mesh,
        in_specs=placed,
        out_specs=(P("dp", "tensor", "seq"), P("dp", "tensor", "seq")),
        check_vma=False,
    )
```

time: 179 us -> 69.2 us (0.39)
  waiting for transfers between devices: 74.2 us -> 0 us
  Pallas kernels: 0 us -> 64.9 us
  local copies, waits for them, and re-layouts: 48.9 us -> 3.42 us
  between operations: 18.1 us -> 0.64 us
  starting transfers between devices: 15.2 us -> 0 us
  other arithmetic: 11.2 us -> 0 us
  matrix products: 10.8 us -> 0 us
    pallas_call x0 -> x1, Pallas kernels: none -> 64.9 us  [local(): pl.pallas_call(functools.partial(kernel, n_seq, n_tensor), out_shape=(out...]
    all_gather x1 -> x0, waiting for transfers between devices: 63.6 us -> none  [local(): lax.all_gather(memory[None], ('seq', 'tensor'), axis=0, tiled=True)]
    reshape x9 -> x0, local copies, waits for them, and re-layouts: 16.2 us -> none  [the longest x6 9.38 us: windows(): block = block.reshape(win_rows, WIN, win_cols, WIN, HEADS, HEAD_DIM)]
    ppermute x1 -> x0, starting transfers between devices: 15.1 us -> none  [shifted(): return lax.ppermute(block, axis, route)]
    dot_general x5 -> x0, matrix products: 10.8 us -> none  [the longest x1 2.52 us: window_block(): jnp.einsum('whqk,whkd->whqd', weights, values_win, preferred_element_type...]
    ppermute x1 -> x0, waiting for transfers between devices: 10.6 us -> none  [shifted(): return lax.ppermute(block, axis, route)]
    gather x2 -> x0, local copies, waits for them, and re-layouts: 10.1 us -> none  [the longest x1 8.4 us: local(): jnp.take(piece_flat, jnp.clip(flat_index, 0, piece_flat.shape[0] - 1), ax...]
    reduce_sum x2 -> x0, other arithmetic: 7.3 us -> none  [the longest x1 4.21 us: window_block(): row_mean = jnp.mean(x_float, axis=-1, keepdims=True)]
  transfers between devices with their start and end apart: 2 -> 0, of which waited for: 2 -> 0; matrix products, arithmetic and copies ran while one was open for 3% -> 0% of each run, Pallas kernels for 0% -> 0%
where the time goes in v1:
time: 69.2 us; the launch traced here: 69 us
  Pallas kernels  64.9 us (94%)
  local copies, waits for them, and re-layouts  3.42 us (5%)
    pallas_call x1, Pallas kernels, local(): pl.pallas_call(functools.partial(kernel, n_seq, n_tensor), out_shape=(out...  64.9 us
    unnamed x2, local copies, waits for them, and re-layouts  3.42 us

profile of v1, /device:TPU:1, one launch (start us, length us, event | category | flops | bytes accessed | tf_op | source)
XLA Modules:
  0.0 69.0 jit_solution(7720375405836483369)
XLA Ops:
  0.6 64.9 %encode_to_kv.1 = (bf16[6,98,256]{2,1,0:T(8,128)(2,1)}, bf16[6,98,256]{2,1,0:T(8,128)(2,1)}) custom-call(s32[1,2]{1,0:T(1,128)} %shift_ref.1, bf16[147,1024]{1,0:T(8,128)(2,1)} %bitcast.2, f32[1,1024]{1,0:T(1,128)} %bitcast.3, s32[6,588]{1,0:T(8,128)} %order_ref.1, bf16[1024,1536]{1,0:T(8,128)(2,1)} %qkv_hbm.1, bf16[512,1024]{1,0:T(8,128)(2,1)} %out_hbm.1, ...), custom_call_target="tpu_custom_call" | custom-call | tf_op jit(solution)/shard_map/encode_to_kv/pallas_call | solution.py:307
  65.6 1.7 %copy.12 = bf16[6,98,256]{2,1,0:T(8,128)(2,1)} copy(bf16[6,98,256]{2,1,0:T(8,128)(2,1)} %get-tuple-element.4) | data formatting | bytes 602112
  67.3 1.7 %copy.13 = bf16[6,98,256]{2,1,0:T(8,128)(2,1)} copy(bf16[6,98,256]{2,1,0:T(8,128)(2,1)} %get-tuple-element.5) | data formatting | bytes 602112
